TPU v7x, 512 devices: a whole 4x4x16 slice. The times are simulated.
512 devices in a mesh: gx: 32 (over z, core), gy: 16 (over y, x).
Axes of the slice: x: 4, y: 4, z: 16, core: 2. Of those that a mesh axis runs over, the one named last changes fastest.
Arguments:
- velocity: float32 [3, 6144, 8192], P(None, 'gx', 'gy'), may hold values from -6 to 6
- row_owner: int32 [32, 64], P('gx'), may hold values from 0 to 15, as said below
- cell_list: int32 [4, 262144], P(None, ('gx', 'gy')), may hold values from 0 to 786431
- weights: float32 [4, 262144], P(None, ('gx', 'gy')), may hold values from 0.05 to 0.5
- offsets: float32 [262144], P(('gx', 'gy')), may hold values from -0.5 to 0.5
- relax_rate: float32 [262144], P(('gx', 'gy')), may hold values from 0.05 to 0.8
- particle_velocity: float32 [3, 262144], P(None, ('gx', 'gy')), may hold values from -6 to 6
- live_counts: int32 [2048], P(('gx', 'gy')), may hold values from 1 to 128, as said below
Outputs:
- gradient: float32 [3, 6144, 8192], P(None, 'gx', 'gy')
- fluid_at_particle: float32 [3, 262144], P(None, ('gx', 'gy'))
- updated_velocity: float32 [3, 262144], P(None, ('gx', 'gy'))
Inputs may be any that keep to these rules, and one draw needn't show every extreme that they name: `row_owner`: for every gx index and every gy index, at most 2 of that device's 4 row blocks name one owner; in every row of devices along gy one owner is named by exactly 2 blocks of every device; every owner is named by some block of the row. `live_counts`: the live particles of a block are its first slots.
All inputs are finite; a program needn't handle non-finite values.
Results may differ from a plain program's by a relative error of at most 0.0029.
Values may be sent and summed in bfloat16 or wider, within the bound.
A program may use at most 128 MiB of HBM per device.

v0:
```python
import math

import jax
import jax.numpy as jnp
from jax import lax
from jax.sharding import PartitionSpec as P

ROWB = 128
PSIZE = 128


R_DECAY = (3.0 - math.sqrt(5.0)) / 2.0
A_COEF = 14.0 / 9.0
B_COEF = 1.0 / 9.0
PRECISION_HIGH = lax.Precision.HIGHEST


def extended(cells, sides, width):
    for axis, dim in sides:
        count = lax.axis_size(axis)
        head = lax.slice_in_dim(cells, 0, width, axis=dim)
        tail = lax.slice_in_dim(cells, cells.shape[dim] - width, cells.shape[dim], axis=dim)
        cells = jnp.concatenate(
            [
                lax.ppermute(tail, axis, [(i, (i + 1) % count) for i in range(count)]),
                cells,
                lax.ppermute(head, axis, [((i + 1) % count, i) for i in range(count)]),
            ],
            axis=dim,
        )
    return cells


def stencil_sum(values, weights, offsets):
    carried = values[:3].astype(jnp.float32)
    slopes = values[3:].astype(jnp.float32)
    return jnp.sum(weights[None] * (carried + offsets[None, None] * slopes), 1)


def pick_cells(table, row_ids, line_ids):
    row_width = table.shape[2]
    picked = jnp.take(table, row_ids.reshape(-1), axis=1)
    select = jnp.arange(row_width)[None, :] == line_ids.reshape(-1)[:, None]
    values = jnp.sum(jnp.where(select[None], picked, jnp.zeros((), table.dtype)), -1)
    return values.reshape((table.shape[0],) + row_ids.shape)


def signed_power(exponent):
    parity = 1.0 - 2.0 * (exponent % 2).astype(jnp.float32)
    return parity * R_DECAY ** exponent.astype(jnp.float32)


def triangle(x_cells, backward):
    position = jnp.arange(x_cells)
    distance = position[:, None] - position[None, :]
    if backward:
        distance = -distance
    return jnp.where(distance >= 0, signed_power(jnp.abs(distance)), 0.0)


def widened_solve(velocity):
    components, x_cells, local_lines = velocity.shape
    margin = 20
    extent = x_cells + 2 * margin
    padded = extended(velocity, (("gx", 1),), margin + 2)
    right_side = 0.5 * A_COEF * (
        padded[:, 3 : extent + 3] - padded[:, 1 : extent + 1]
    ) + 0.25 * B_COEF * (padded[:, 4 : extent + 4] - padded[:, 0:extent])
    forward = jnp.einsum(
        "ij,cjl->cil", triangle(extent, False), right_side, precision=PRECISION_HIGH
    )
    backward = jnp.einsum("ij,cjl->cil", triangle(extent, True), forward, precision=PRECISION_HIGH)
    return 3.0 * R_DECAY * backward[:, margin : margin + x_cells]


def per_device(
    velocity, row_owner, cell_list, weights, offsets, relax_rate, particle_velocity, live_counts
):
    components, x_cells, local_lines = velocity.shape
    gradient = widened_solve(velocity)
    fields = jnp.concatenate([velocity, gradient], 0).astype(jnp.bfloat16)
    my_owner = lax.axis_index("gy")
    owners = lax.axis_size("gy")
    block_total = local_lines // ROWB
    capacity = block_total // 2
    column = row_owner[0]
    x_index = cell_list % x_cells
    remainder = cell_list // x_cells
    line_index = remainder % ROWB
    slot_ids = remainder // ROWB
    own_routes = lax.dynamic_slice_in_dim(column, my_owner * block_total, block_total)
    ordinal = jnp.arange(block_total)
    earlier_same = (own_routes[:, None] == own_routes[None, :]) & (
        ordinal[None, :] < ordinal[:, None]
    )
    ranking = jnp.sum(earlier_same.astype(jnp.int32), 1)
    slot_index = own_routes * capacity + ranking
    matches = (slot_index[None, :] == jnp.arange(owners * capacity)[:, None]).astype(jnp.bfloat16)
    blocked = fields.reshape(6, x_cells, block_total, ROWB)
    outgoing = jnp.einsum("ckbr,sb->cksr", blocked, matches, preferred_element_type=jnp.bfloat16)
    outgoing = outgoing.reshape(6, x_cells, owners, capacity, ROWB)
    arrived = lax.all_to_all(outgoing, "gy", split_axis=2, concat_axis=2, tiled=True)
    table = arrived.reshape(6, x_cells * owners * capacity, ROWB)
    row_ids = x_index * (owners * capacity) + slot_ids
    raw = stencil_sum(pick_cells(table, row_ids, line_index), weights, offsets)
    particle_slots = weights.shape[1]
    alive = (jnp.arange(PSIZE)[None, :] < live_counts[:, None]).reshape(particle_slots)
    fluid_at_particle = jnp.where(alive[None], raw, 0.0)
    updated_velocity = jnp.where(
        alive[None],
        particle_velocity + relax_rate[None] * (fluid_at_particle - particle_velocity),
        particle_velocity,
    )
    return (gradient, fluid_at_particle, updated_velocity)


def solution(mesh):
    return jax.shard_map(
        per_device,
        mesh=mesh,
        in_specs=(
            P(None, "gx", "gy"),
            P("gx", None),
            P(None, ("gx", "gy")),
            P(None, ("gx", "gy")),
            P(("gx", "gy")),
            P(("gx", "gy")),
            P(None, ("gx", "gy")),
            P(("gx", "gy")),
        ),
        out_specs=(P(None, "gx", "gy"), P(None, ("gx", "gy")), P(None, ("gx", "gy"))),
        check_vma=False,
    )
```

profile of v0, /device:TPU:289, one launch (start us, length us, event | category | flops | bytes accessed | tf_op | source)
XLA Modules:
  0.0 247.8 jit_solution(14806160395370510572)
XLA Ops:
  0.6 0.0 copy-start.6
  0.6 1.0 fusion.99
  1.7 1.3 collective-permute-start
  3.0 0.0 collective-permute-start.1
  3.0 0.0 copy-start
  3.0 1.4 convert.11
  4.4 0.0 copy-done.6
  4.4 0.1 fusion.82
  4.5 0.2 convert_reduce_fusion
  4.7 0.1 concatenate.13
  4.8 0.1 fusion.79
  4.9 0.2 collective-permute-done
  5.1 2.5 collective-permute-done.1
  7.5 0.0 copy-done
  7.5 0.2 pad_maximum_fusion
  7.7 2.0 convolution_bitcast_fusion.1
  9.8 1.5 convolution_bitcast_fusion
  11.3 1.2 fusion.98
  12.6 0.1 concatenate.14
  12.7 3.1 %fusion.7 = bf16[32,6,192,128]{3,0,2,1:T(8,128)(2,1)S(1)} fusion(bf16[3,192,4,128]{3,2,1,0:T(4,128)(2,1)S(1)} %concatenate.14, bf16[3,192,4,128]{3,2,1,0:T(4,128)(2,1)S(1)} %concatenate.13, s32[4]{0:T(128)S(1)} %fusion.79), kind=kOutput, calls=%fused_computation.13 | convolution fusion | flops 40108160 | bytes 10616848 | tf_op jit(solution)/shard_map/ckbr,sb->cksr/dot_general | solution.py:100
  15.8 10.2 %copy.30 = bf16[6,192,16,2,128]{4,3,1,0,2:T(2,128)(2,1)} copy(bf16[6,192,16,2,128]{4,3,2,1,0:T(2,128)(2,1)S(1)} %bitcast.45) | data formatting | bytes 18874368 | tf_op jit(solution)/shard_map/reshape | solution.py:101
  26.0 0.0 copy-start.2
  26.0 0.0 copy-start.7
  26.0 6.9 %all-to-all-start = ((bf16[6,192,16,2,128]{4,3,1,0,2:T(2,128)(2,1)}), bf16[6,192,16,2,128]{4,3,1,0,2:T(2,128)(2,1)}, u32[]{:S(2)}, u32[]{:S(2)}) async-start(bf16[6,192,16,2,128]{4,3,1,0,2:T(2,128)(2,1)} %copy.30), calls=%async_computation | async-start | bytes 18874368 | tf_op jit(solution)/shard_map/all_to_all | solution.py:102
  33.0 0.0 copy-done.2
  33.1 0.0 copy-done.7
  33.1 0.1 fusion.74
  33.2 0.3 iota_compare_fusion
  33.5 144.0 %all-to-all-done = bf16[6,192,16,2,128]{4,3,1,0,2:T(2,128)(2,1)} async-done(((bf16[6,192,16,2,128]{4,3,1,0,2:T(2,128)(2,1)}), bf16[6,192,16,2,128]{4,3,1,0,2:T(2,128)(2,1)}, u32[]{:S(2)}, u32[]{:S(2)}) %all-to-all-start) | async-done | bytes 9437216 | tf_op jit(solution)/shard_map/all_to_all | solution.py:102
  177.6 19.0 %copy.31 = bf16[6,192,16,2,128]{4,0,3,2,1:T(8,128)(2,1)} copy(bf16[6,192,16,2,128]{4,3,1,0,2:T(2,128)(2,1)} %all-to-all-done) | data formatting | bytes 18874368 | tf_op jit(solution)/shard_map/all_to_all | solution.py:102
  196.6 19.3 %gather_fusion = bf16[2048,6,128]{2,1,0:T(8,128)(2,1)} fusion(bf16[6,6144,128]{2,0,1:T(8,128)(2,1)} %bitcast.46, s32[2048]{0:T(1024)S(1)} %broadcast_clamp_fusion), kind=kCustom, calls=%fused_computation | custom fusion | bytes 6299648 | tf_op jit(solution)/shard_map/jit(_take)/gather | solution.py:42
  215.9 30.1 %select_reduce_fusion = bf16[2048,6]{1,0:T(8,128)(2,1)S(1)} fusion(bf16[2048,6,128]{2,1,0:T(8,128)(2,1)} %gather_fusion, pred[2048]{0:T(1024)(128)(4,1)S(1)} %compare_and_fusion, pred[2048,128]{1,0:T(8,128)(4,1)S(1)} %iota_compare_fusion), kind=kLoop, calls=%fused_computation.1 | loop fusion | flops 4706304 | bytes 3434496 | tf_op jit(solution)/shard_map/reduce_sum | solution.py:44
  245.9 0.0 copy-start.1
  245.9 0.0 copy-start.4
  246.0 0.0 copy-start.3
  246.0 0.0 copy-start.5
  246.0 0.2 fusion.100
  246.2 0.4 copy-done.1
  246.6 0.0 copy-done.4
  246.6 0.4 fusion.13
  247.0 0.1 copy.32
  247.2 0.0 copy-done.3
  247.2 0.0 copy-done.5
  247.2 0.6 add_select_fusion.2
  (7 shorter events, 0.1 us)
Async XLA Ops:
  0.6 3.8 %copy-start.6 = (s32[1,64]{1,0:T(1,128)S(1)}, s32[1,64]{1,0:T(1,128)}, u32[]{:S(2)}) copy-start(s32[1,64]{1,0:T(1,128)} %param.9) | copy-start | bytes 772
  1.7 3.4 %collective-permute-start = (f32[3,22,512]{2,1,0:T(8,128)S(1)}, f32[3,22,512]{2,1,0:T(8,128)S(1)}, u32[]{:S(2)}, u32[]{:S(2)}) collective-permute-start(f32[3,22,512]{2,1,0:T(8,128)S(1)} %get-tuple-element.13), channel_id=1, source_target_pairs={{0,16},{16,32},{32,48},{48,64},{64,80},{80,96},{96,112},{112,128},... | collective-permute-start | bytes 405512 | tf_op jit(solution)/shard_map/ppermute | solution.py:25
  3.0 4.6 %collective-permute-start.1 = (f32[3,22,512]{2,1,0:T(8,128)S(1)}, f32[3,22,512]{2,1,0:T(8,128)S(1)}, u32[]{:S(2)}, u32[]{:S(2)}) collective-permute-start(f32[3,22,512]{2,1,0:T(8,128)S(1)} %get-tuple-element.14), channel_id=1, source_target_pairs={{16,0},{32,16},{48,32},{64,48},{80,64},{96,80},{112,96},{128,112},... | collective-permute-start | bytes 405512 | tf_op jit(solution)/shard_map/ppermute | solution.py:27
  3.0 4.6 %copy-start = (f32[3,192,512]{2,1,0:T(8,128)S(1)}, f32[3,192,512]{2,1,0:T(8,128)}, u32[]{:S(2)}) copy-start(f32[3,192,512]{2,1,0:T(8,128)} %param.8) | copy-start | bytes 3538948
  26.0 7.0 %copy-start.2 = (s32[4,512]{1,0:T(4,128)S(1)}, s32[4,512]{1,0:T(4,128)}, u32[]{:S(2)}) copy-start(s32[4,512]{1,0:T(4,128)} %param.10) | copy-start | bytes 24580
  26.0 7.0 %copy-start.7 = (s32[4]{0:T(128)S(1)}, s32[4]{0:T(128)}, u32[]{:S(2)}) copy-start(s32[4]{0:T(128)} %param.15) | copy-start | bytes 52
  26.0 151.5 %all-to-all-start = ((bf16[6,192,16,2,128]{4,3,1,0,2:T(2,128)(2,1)}), bf16[6,192,16,2,128]{4,3,1,0,2:T(2,128)(2,1)}, u32[]{:S(2)}, u32[]{:S(2)}) async-start(bf16[6,192,16,2,128]{4,3,1,0,2:T(2,128)(2,1)} %copy.30), calls=%async_computation | async-start | bytes 18874368 | tf_op jit(solution)/shard_map/all_to_all | solution.py:102
  245.9 0.7 copy-start.1
  245.9 0.7 copy-start.4
  246.0 1.2 copy-start.3
  246.0 1.2 copy-start.5
where the time goes:
time: 248 us
  waiting for transfers between devices  147 us (59%)
  local copies, waits for them, and re-layouts  50.7 us (20%)
  other arithmetic  34.7 us (14%)
  starting transfers between devices  8.26 us (3%)
  matrix products  6.66 us (3%)
    all_to_all x1, waiting for transfers between devices, per_device(): lax.all_to_all(outgoing, 'gy', split_axis=2, concat_axis=2, tiled=True)  144 us
    reduce_sum x1, other arithmetic, pick_cells(): jnp.sum(jnp.where(select[None], picked, jnp.zeros((), table.dtype)), -1)  30.1 us
    gather x1, local copies, waits for them, and re-layouts, pick_cells(): picked = jnp.take(table, row_ids.reshape(-1), axis=1)  19.3 us
    all_to_all x1, local copies, waits for them, and re-layouts, per_device(): lax.all_to_all(outgoing, 'gy', split_axis=2, concat_axis=2, tiled=True)  19 us
    reshape x1, local copies, waits for them, and re-layouts, per_device(): outgoing = outgoing.reshape(6, x_cells, owners, capacity, ROWB)  10.2 us
    all_to_all x1, starting transfers between devices, per_device(): lax.all_to_all(outgoing, 'gy', split_axis=2, concat_axis=2, tiled=True)  6.94 us
  transfers between devices with their start and end apart: 3, of which 3 were waited for; matrix products, arithmetic and copies ran while one was open for 1% of the time, Pallas kernels for 0%

commit v1 on v0

v1 whole, which is shorter than its diff:
```python
import functools
import math

import jax
import jax.numpy as jnp
import numpy as np
from jax import lax
from jax.experimental import pallas as pl
from jax.experimental.pallas import tpu as pltpu
from jax.sharding import PartitionSpec as P

ROWB = 128
PSIZE = 128
CAP = 2
STEN = 4
XSPLIT = 4
MESH = pl.DeviceIdType.MESH

DECAY = (3.0 - math.sqrt(5.0)) / 2.0
RATIO = -DECAY
GAIN = 3.0 / math.sqrt(5.0)


def green(distance):
    return GAIN * RATIO ** abs(distance)


def response(d):
    return (7.0 / 9.0) * (green(d + 1) - green(d - 1)) + (1.0 / 36.0) * (green(d + 2) - green(d - 2))


TAIL = response(2) / RATIO**2
NEAR = response(1) - TAIL * RATIO


def response_matrix(x_cells):
    table = np.array([response(d) for d in range(1 - x_cells, x_cells)])
    position = np.arange(x_cells)
    exact = table[position[:, None] - position[None, :] + x_cells - 1]
    high = exact.astype(jnp.bfloat16)
    low = (exact - high.astype(np.float64)).astype(jnp.bfloat16)
    return np.stack([high, low])


def decay_table(x_cells):
    position = np.arange(x_cells)
    powers = RATIO ** np.minimum(position, x_cells - 1 - position).astype(np.float64)
    return np.broadcast_to(powers[:, None], (x_cells, ROWB)).astype(np.float32)


def third(value):
    return lax.shift_right_logical(value * 43691, 17)


def kernel(
    ring,
    side,
    owner_ref,
    vel_ref,
    cells_ref,
    weights_ref,
    offsets_ref,
    matrix_ref,
    decay_ref,
    grad,
    raw_ref,
    owners,
    vel,
    matrix,
    decay,
    fields,
    halo_out,
    halo_in,
    cells,
    weights,
    offsets,
    picked,
    back_out,
    back_in,
    load_sem,
    halo_send,
    halo_recv,
    cell_send,
    cell_recv,
    weight_send,
    weight_recv,
    offset_send,
    offset_recv,
    back_send,
    back_recv,
):
    components, x_cells, lines = vel.shape
    blocks = lines // ROWB
    half = x_cells // 2
    run = x_cells // XSPLIT
    particles = cells.shape[-1]
    peers = side * side
    col = lax.axis_index("gx")
    row = lax.axis_index("gy")
    row_y, row_x = lax.div(row, side), lax.rem(row, side)
    right, left = lax.rem(col + 1, ring), lax.rem(col + ring - 1, ring)

    def peer(step):
        y = lax.rem(row_y + lax.div(step, side), side)
        x = lax.rem(row_x + lax.rem(step, side), side)
        return y * side + x

    barrier = pltpu.get_barrier_semaphore()
    for neighbour in (left, right):
        pl.semaphore_signal(barrier, inc=1, device_id=(neighbour, row), device_id_type=MESH)

    @pl.loop(1, peers)
    def _(step):
        pl.semaphore_signal(barrier, inc=1, device_id=(col, peer(step)), device_id_type=MESH)

    loads = [
        pltpu.make_async_copy(source, target, load_sem.at[i])
        for i, (source, target) in enumerate(
            (
                (vel_ref, vel),
                (decay_ref, decay),
                (cells_ref, cells.at[0]),
                (weights_ref, weights.at[0]),
                (offsets_ref, offsets.at[0]),
                (matrix_ref, matrix),
                (owner_ref, owners),
            )
        )
    ]
    for load in loads:
        load.start()

    loads[0].wait()
    loads[1].wait()
    for c in range(components):
        for b in range(blocks):
            lanes = slice(b * ROWB, (b + 1) * ROWB)
            halo_out[0, c : c + 1, lanes] = jnp.sum(
                vel[c, half:, lanes] * decay[half:, :], 0, keepdims=True
            )
            halo_out[1, c : c + 1, lanes] = jnp.sum(
                vel[c, :half, lanes] * decay[:half, :], 0, keepdims=True
            )
        halo_out[0, 4 + c : 5 + c, :] = vel[c, x_cells - 1 : x_cells, :]
        halo_out[1, 4 + c : 5 + c, :] = vel[c, 0:1, :]
    for load in loads[2:]:
        load.wait()

    def halo_copy(way, target):
        return pltpu.make_async_remote_copy(
            src_ref=halo_out.at[way],
            dst_ref=halo_in.at[way],
            send_sem=halo_send.at[way],
            recv_sem=halo_recv.at[way],
            device_id=(target, row),
            device_id_type=MESH,
        )

    def share(array, step, send_sem, recv_sem):
        return pltpu.make_async_remote_copy(
            src_ref=array.at[0],
            dst_ref=array.at[step],
            send_sem=send_sem.at[step],
            recv_sem=recv_sem.at[step],
            device_id=(col, peer(step)),
            device_id_type=MESH,
        )

    def give_back(step):
        return pltpu.make_async_remote_copy(
            src_ref=back_out.at[step],
            dst_ref=back_in.at[step],
            send_sem=back_send.at[step],
            recv_sem=back_recv.at[step],
            device_id=(col, peer(step)),
            device_id_type=MESH,
        )

    shared = (
        (cells, cell_send, cell_recv),
        (weights, weight_send, weight_recv),
        (offsets, offset_send, offset_recv),
    )
    pl.semaphore_wait(barrier, peers + 1)
    halos = [halo_copy(0, right), halo_copy(1, left)]
    for halo in halos:
        halo.start()
    for entry in shared:

        @pl.loop(1, peers)
        def _(step, entry=entry):
            array, send_sem, recv_sem = entry
            share(array, step, send_sem, recv_sem).start()

    for c in range(components):
        value = vel[c]
        high = value.astype(jnp.bfloat16)
        low = (value - high.astype(jnp.float32)).astype(jnp.bfloat16)
        dot = functools.partial(jnp.dot, preferred_element_type=jnp.float32)
        grad[c] = dot(matrix[0], high) + (dot(matrix[0], low) + dot(matrix[1], high))
        for b in range(blocks):
            lanes = slice(b * ROWB, (b + 1) * ROWB)
            for k in range(XSPLIT):
                fields[b, c * run : (c + 1) * run, k * ROWB : (k + 1) * ROWB] = high[
                    k * run : (k + 1) * run, lanes
                ]

    for halo in halos:
        halo.wait_recv()
    for c in range(components):
        for end, way, sign in ((0, 0, 1.0), (x_cells - 1, 1, -1.0)):
            grad[c, end : end + 1, :] += (sign * NEAR) * halo_in[way, 4 + c : 5 + c, :]
        for b in range(blocks):
            lanes = slice(b * ROWB, (b + 1) * ROWB)
            for way, sign in ((0, 1.0), (1, -1.0)):
                rows = slice(way * half, (way + 1) * half)
                far = (sign * TAIL * RATIO) * halo_in[way, c : c + 1, lanes]
                total = grad[c, rows, lanes] + decay[rows, :] * far
                grad[c, rows, lanes] = total
                rounded = total.astype(jnp.bfloat16)
                for k in range(XSPLIT // 2):
                    place = way * (XSPLIT // 2) + k
                    fields[
                        b,
                        (components + c) * run : (components + c + 1) * run,
                        place * ROWB : (place + 1) * ROWB,
                    ] = rounded[k * run : (k + 1) * run]

    for array, send_sem, recv_sem in shared:

        @pl.loop(1, peers)
        def _(step, entry=(array, send_sem, recv_sem)):
            array, send_sem, recv_sem = entry
            share(array, step, send_sem, recv_sem).wait()

    owner_of = [owners[0, row * blocks + b] for b in range(blocks)]
    depth = XSPLIT * ROWB
    place_id = lax.broadcasted_iota(jnp.int32, (256, particles), 0).astype(jnp.bfloat16)
    run_id = lax.broadcasted_iota(jnp.int32, (run, particles), 0)
    one, zero = jnp.ones((), jnp.bfloat16), jnp.zeros((), jnp.bfloat16)

    @pl.loop(0, blocks)
    def _(b):
        owner = owners[0, row * blocks + b]
        rank = jnp.int32(0)
        for other in range(blocks):
            same = jnp.where(owner_of[other] == owner, 1, 0)
            rank += same * jnp.where(other < b, 1, 0)
        slot_y = lax.rem(row_y - lax.div(owner, side) + side, side)
        slot_x = lax.rem(row_x - lax.rem(owner, side) + side, side)
        slot = slot_y * side + slot_x
        cell = cells[slot]
        weight = weights[slot]
        offset = offsets[slot]
        line = third(lax.shift_right_logical(cell, 6))
        x = cell - line * x_cells
        source = lax.shift_right_logical(line, 7)
        line = line & (ROWB - 1)
        part = third(lax.shift_right_logical(x, (run // 3).bit_length() - 1))
        within = x - part * run
        place = part * ROWB + line
        sums = [jnp.zeros((8, particles), jnp.float32) for _ in range(components)]
        table = fields[b]
        for s in range(STEN):
            hot = []
            for start in range(0, depth, 256):
                key = (place[s : s + 1] - start).astype(jnp.bfloat16)
                hot.append(jnp.where(place_id == key, one, zero))
            values = jnp.dot(
                table, jnp.concatenate(hot, 0), preferred_element_type=jnp.float32
            )
            chosen = run_id == within[s : s + 1]
            parts = []
            for f in range(2 * components):
                kept = jnp.where(chosen, values[f * run : (f + 1) * run], 0.0)
                parts.append(jnp.sum(kept.reshape(run // 8, 8, particles), 0))
            for c in range(components):
                sums[c] += weight[s : s + 1] * (parts[c] + offset * parts[components + c])
        mine = source[0:1] == row * CAP + rank
        for c in range(components):
            total = jnp.sum(sums[c], 0, keepdims=True)
            picked[b, c : c + 1, :] = jnp.where(mine, total, 0.0)

    @pl.loop(0, peers)
    def _(step):
        to = peer(step)
        total = jnp.zeros(picked.shape[1:], jnp.float32)
        for b in range(blocks):
            total += picked[b] * jnp.where(owner_of[b] == to, 1.0, 0.0)
        back_out[step] = total

    @pl.loop(1, peers)
    def _(step):
        give_back(step).start()

    @pl.loop(1, peers)
    def _(step):
        give_back(step).wait()

    total = back_out[0]
    for step in range(1, peers):
        total += back_in[step]
    raw_ref[...] = total
    for halo in halos:
        halo.wait_send()


def per_device(
    ring,
    side,
    velocity,
    row_owner,
    cell_list,
    weights,
    offsets,
    relax_rate,
    particle_velocity,
    live_counts,
):
    components, x_cells, lines = velocity.shape
    blocks = lines // ROWB
    particles = weights.shape[1]
    peers = side * side
    run = x_cells // XSPLIT
    far = pl.BlockSpec(memory_space=pltpu.HBM)
    near = pl.BlockSpec(memory_space=pltpu.VMEM)
    dma = pltpu.SemaphoreType.DMA
    gradient, raw = pl.pallas_call(
        functools.partial(kernel, ring, side),
        out_shape=(
            jax.ShapeDtypeStruct(velocity.shape, jnp.float32),
            jax.ShapeDtypeStruct((components, particles), jnp.float32),
        ),
        in_specs=[far] * 7,
        out_specs=(near, near),
        scratch_shapes=[
            pltpu.SMEM(row_owner.shape, jnp.int32),
            pltpu.VMEM(velocity.shape, jnp.float32),
            pltpu.VMEM((2, x_cells, x_cells), jnp.bfloat16),
            pltpu.VMEM((x_cells, ROWB), jnp.float32),
            pltpu.VMEM((blocks, 2 * components * run, XSPLIT * ROWB), jnp.bfloat16),
            pltpu.VMEM((2, 8, lines), jnp.float32),
            pltpu.VMEM((2, 8, lines), jnp.float32),
            pltpu.VMEM((peers, STEN, particles), jnp.int32),
            pltpu.VMEM((peers, STEN, particles), jnp.float32),
            pltpu.VMEM((peers, 1, particles), jnp.float32),
            pltpu.VMEM((blocks, components, particles), jnp.float32),
            pltpu.VMEM((peers, components, particles), jnp.float32),
            pltpu.VMEM((peers, components, particles), jnp.float32),
            dma((7,)),
            dma((2,)),
            dma((2,)),
        ]
        + [dma((peers,))] * 8,
        compiler_params=pltpu.CompilerParams(
            collective_id=0, has_side_effects=True, vmem_limit_bytes=48 * 1024 * 1024
        ),
    )(
        *(
            pltpu.with_memory_space_constraint(array, pltpu.HBM)
            for array in (
                row_owner,
                velocity,
                cell_list,
                weights,
                offsets[None],
                jnp.asarray(response_matrix(x_cells)),
                jnp.asarray(decay_table(x_cells)),
            )
        ),
    )
    alive = (jnp.arange(PSIZE)[None, :] < live_counts[:, None]).reshape(particles)
    fluid_at_particle = jnp.where(alive[None], raw, 0.0)
    updated_velocity = jnp.where(
        alive[None],
        particle_velocity + relax_rate[None] * (fluid_at_particle - particle_velocity),
        particle_velocity,
    )
    return gradient, fluid_at_particle, updated_velocity


def solution(mesh):
    side = math.isqrt(mesh.shape["gy"])
    return jax.shard_map(
        functools.partial(per_device, mesh.shape["gx"], side),
        mesh=mesh,
        in_specs=(
            P(None, "gx", "gy"),
            P("gx", None),
            P(None, ("gx", "gy")),
            P(None, ("gx", "gy")),
            P(("gx", "gy")),
            P(("gx", "gy")),
            P(None, ("gx", "gy")),
            P(("gx", "gy")),
        ),
        out_specs=(P(None, "gx", "gy"), P(None, ("gx", "gy")), P(None, ("gx", "gy"))),
        check_vma=False,
    )
```

time: 248 us -> 29.3 us (0.12)
  the two profiles are of different devices: /device:TPU:289 before, /device:TPU:4 now
where the time goes in v1:
time: 29.3 us; the launch traced here: 29.2 us
  Pallas kernels  26.8 us (91%)
  local copies, waits for them, and re-layouts  1.03 us (4%)
  other arithmetic  0.68 us (2%)
  between operations  0.68 us (2%)
    pallas_call x1, Pallas kernels, per_device(): pl.pallas_call(functools.partial(kernel, ring, side), out_shape=(jax.Shap...  26.8 us
    unnamed x7, local copies, waits for them, and re-layouts  1.03 us
    select_n x1, other arithmetic, per_device(): jnp.where(alive[None], particle_velocity + relax_rate[None] * (fluid_at_p...  0.61 us

profile of v1, /device:TPU:4, one launch (start us, length us, event | category | flops | bytes accessed | tf_op | source)
XLA Modules:
  0.0 29.2 jit_solution(9992402400200379412)
XLA Ops:
  0.6 0.0 copy-start
  0.6 0.0 copy-start.1
  0.7 0.0 copy-start.2
  0.7 26.8 %shard_map.121 = (f32[3,192,512]{2,1,0:T(8,128)S(1)}, f32[3,512]{1,0:T(4,128)S(1)}) custom-call(s32[1,64]{1,0:T(1,128)} %owner_ref.1, f32[3,192,512]{2,1,0:T(8,128)} %vel_ref.1, s32[4,512]{1,0:T(4,128)} %cells_ref.1, f32[4,512]{1,0:T(4,128)} %weights_ref.1, f32[1,512]{1,0:T(1,128)} %bitcast.3, bf16[2,192,192]{2,1,0:T(8,128)(2,1)} %constant.6.clone.matrix_ref, ...), custom_call_target="tpu_custom_call" | custom-call | tf_op jit(solution)/shard_map/pallas_call | solution.py:328
  27.4 0.0 copy-done.2
  27.5 0.1 fusion
  27.5 0.0 copy-done
  27.5 0.0 copy-done.1
  27.5 0.6 %add_select_fusion = (f32[3,512]{1,0:T(4,128)}, f32[3,512]{1,0:T(4,128)}) fusion(f32[3,512]{1,0:T(4,128)S(1)} %copy-done, f32[512]{0:T(512)S(1)} %copy-done.1, pred[512]{0:T(512)(128)(4,1)S(1)} %fusion, f32[3,512]{1,0:T(4,128)S(1)} %get-tuple-element.6), kind=kLoop, calls=%fused_computation | loop fusion | flops 7680 | bytes 27136 | tf_op jit(solution)/shard_map/jit(_where)/select_n | solution.py:374
  28.1 1.0 %copy.14 = f32[3,192,512]{2,1,0:T(8,128)} copy(f32[3,192,512]{2,1,0:T(8,128)S(1)} %get-tuple-element.12) | data formatting | bytes 2359296
Async XLA Ops:
  0.6 26.9 %copy-start = (f32[3,512]{1,0:T(4,128)S(1)}, f32[3,512]{1,0:T(4,128)}, u32[]{:S(2)}) copy-start(f32[3,512]{1,0:T(4,128)} %param.16) | copy-start | bytes 18436
  0.6 26.9 %copy-start.1 = (f32[512]{0:T(512)S(1)}, f32[512]{0:T(512)}, u32[]{:S(2)}) copy-start(f32[512]{0:T(512)} %param.15) | copy-start | bytes 6148
  0.7 26.8 %copy-start.2 = (s32[4]{0:T(128)S(1)}, s32[4]{0:T(128)}, u32[]{:S(2)}) copy-start(s32[4]{0:T(128)} %param.17) | copy-start | bytes 52

commit v2 on v1

v2 whole, which is shorter than its diff:
```python
import functools
import math

import jax
import jax.numpy as jnp
import numpy as np
from jax import lax
from jax.experimental import pallas as pl
from jax.experimental.pallas import tpu as pltpu
from jax.sharding import PartitionSpec as P

ROWB = 128
PSIZE = 128
CAP = 2
STEN = 4
XSPLIT = 4
MESH = pl.DeviceIdType.MESH

DECAY = (3.0 - math.sqrt(5.0)) / 2.0
RATIO = -DECAY
GAIN = 3.0 / math.sqrt(5.0)


def green(distance):
    return GAIN * RATIO ** abs(distance)


def response(d):
    return (7.0 / 9.0) * (green(d + 1) - green(d - 1)) + (1.0 / 36.0) * (green(d + 2) - green(d - 2))


TAIL = response(2) / RATIO**2
NEAR = response(1) - TAIL * RATIO


def response_matrix(x_cells):
    table = np.array([response(d) for d in range(1 - x_cells, x_cells)])
    position = np.arange(x_cells)
    exact = table[position[:, None] - position[None, :] + x_cells - 1]
    high = exact.astype(jnp.bfloat16)
    low = (exact - high.astype(np.float64)).astype(jnp.bfloat16)
    return np.stack([high, low])


def decay_table(x_cells):
    position = np.arange(x_cells)
    powers = RATIO ** np.minimum(position, x_cells - 1 - position).astype(np.float64)
    return np.broadcast_to(powers[:, None], (x_cells, ROWB)).astype(np.float32)


def third(value):
    return lax.shift_right_logical(value * 43691, 17)


def is_equal(value, other):
    return jnp.where(value == other, 1, 0)


def kernel(
    ring,
    side,
    owner_ref,
    vel_ref,
    cells_ref,
    weights_ref,
    offsets_ref,
    relax_ref,
    particle_ref,
    live_ref,
    matrix_ref,
    decay_ref,
    grad,
    fluid,
    updated,
    owners,
    vel,
    matrix,
    decay,
    carried,
    slopes,
    hot,
    halo_out,
    halo_in,
    cells,
    weights,
    offsets,
    relax,
    particle,
    live,
    picked,
    result,
    back_out,
    back_in,
    ready,
    load_sem,
    halo_send,
    halo_recv,
    cell_send,
    cell_recv,
    weight_send,
    weight_recv,
    offset_send,
    offset_recv,
    back_send,
    back_recv,
):
    components, x_cells, lines = vel.shape
    blocks = lines // ROWB
    run = x_cells // XSPLIT
    particles = cells.shape[-1]
    peers = side * side
    col = lax.axis_index("gx")
    row = lax.axis_index("gy")
    row_y, row_x = lax.div(row, side), lax.rem(row, side)
    right, left = lax.rem(col + 1, ring), lax.rem(col + ring - 1, ring)

    def peer(step):
        y = lax.rem(row_y + lax.div(step, side), side)
        x = lax.rem(row_x + lax.rem(step, side), side)
        return y * side + x

    near_first = sorted(range(1, side), key=lambda k: -min(k, side - k))

    odd = lax.rem(col, 2)
    first, last, second = is_equal(col, 0), is_equal(col, ring - 1), is_equal(col, 1)
    leads = (
        first + odd * (1 - last) * (1 - first),
        first + odd * (1 - second) * (1 - first),
    )
    beside = (right, left)

    barrier = pltpu.get_barrier_semaphore()

    for k in near_first:
        for step in (k, k * side):
            pl.semaphore_signal(
                barrier, inc=1, device_id=(col, peer(step)), device_id_type=MESH
            )
    for way in range(2):

        @pl.when(leads[way] == 1)
        def _(way=way):
            pl.semaphore_signal(
                barrier, inc=1, device_id=(beside[way], row), device_id_type=MESH
            )

    edge = (slice(0, run), slice(x_cells - run, x_cells))
    inner = slice(run, x_cells - run)
    loads = [
        pltpu.make_async_copy(source, target, load_sem.at[i])
        for i, (source, target) in enumerate(
            (
                (decay_ref, decay),
                (vel_ref.at[:, edge[0]], vel.at[:, edge[0]]),
                (vel_ref.at[:, edge[1]], vel.at[:, edge[1]]),
                (cells_ref, cells.at[0, 0]),
                (weights_ref, weights.at[0, 0]),
                (offsets_ref, offsets.at[0, 0]),
                (vel_ref.at[:, inner], vel.at[:, inner]),
                (matrix_ref, matrix),
                (owner_ref, owners),
                (relax_ref, relax),
                (particle_ref, particle),
                (live_ref, live),
            )
        )
    ]
    for load in loads:
        load.start()

    def halo_copy(way):
        return pltpu.make_async_remote_copy(
            src_ref=halo_out.at[way],
            dst_ref=halo_in.at[way],
            send_sem=halo_send.at[way],
            recv_sem=halo_recv.at[way],
            device_id=(beside[way], row),
            device_id_type=MESH,
        )

    def share(entry, k):
        source, array, first, send_sem, recv_sem = entry
        return pltpu.make_async_remote_copy(
            src_ref=source,
            dst_ref=array.at[0, k],
            send_sem=send_sem.at[0, k],
            recv_sem=recv_sem.at[0, k],
            device_id=(col, peer(k * first)),
            device_id_type=MESH,
        )

    def share_line(entry, k):
        _, array, first, send_sem, recv_sem = entry
        return pltpu.make_async_remote_copy(
            src_ref=array.at[0],
            dst_ref=array.at[k],
            send_sem=send_sem.at[1, k],
            recv_sem=recv_sem.at[1, k],
            device_id=(col, peer(k * side // first)),
            device_id_type=MESH,
        )

    def give_back(step):
        return pltpu.make_async_remote_copy(
            src_ref=back_out.at[step],
            dst_ref=back_in.at[step],
            send_sem=back_send.at[step],
            recv_sem=back_recv.at[step],
            device_id=(col, peer(step)),
            device_id_type=MESH,
        )

    def hops(step):
        return sum(min(k, side - k) for k in divmod(step, side))

    farthest_first = sorted(range(1, peers), key=hops, reverse=True)
    shared = (
        (cells_ref, cells, 1, cell_send, cell_recv),
        (weights_ref, weights, side, weight_send, weight_recv),
        (offsets_ref, offsets, side, offset_send, offset_recv),
    )
    pl.semaphore_wait(barrier, 2 * (side - 1) + 2 - leads[0] - leads[1])
    for entry in shared:
        for k in near_first:
            share(entry, k).start()
    for way in range(2):

        @pl.when(leads[way] == 0)
        def _(way=way):
            pl.semaphore_signal(
                ready.at[1 - way], inc=1, device_id=(beside[way], row), device_id_type=MESH
            )

    for load in loads[:3]:
        load.wait()
    for c in range(components):
        for b in range(blocks):
            lanes = slice(b * ROWB, (b + 1) * ROWB)
            for way in range(2):
                rows = edge[1 - way]
                halo_out[way, c : c + 1, lanes] = jnp.sum(
                    vel[c, rows, lanes] * decay[rows, :], 0, keepdims=True
                )
        halo_out[0, 4 + c : 5 + c, :] = vel[c, x_cells - 1 : x_cells, :]
        halo_out[1, 4 + c : 5 + c, :] = vel[c, 0:1, :]

    for way in range(2):

        @pl.when(leads[way] == 0)
        def _(way=way):
            halo_copy(way).start()

    for load in loads[3:6]:
        load.wait()
    for entry in shared:
        for k in near_first:
            share(entry, k).wait_recv()
        for k in near_first:
            share_line(entry, k).start()

    for way in range(2):

        @pl.when(leads[way] == 1)
        def _(way=way):
            pl.semaphore_wait(ready.at[way], 1)
            halo_copy(way).start()

    for load in loads[6:]:
        load.wait()
    for c in range(components):
        value = vel[c]
        high = value.astype(jnp.bfloat16)
        low = (value - high.astype(jnp.float32)).astype(jnp.bfloat16)
        dot = functools.partial(jnp.dot, preferred_element_type=jnp.float32)
        total = dot(matrix[0], high) + (dot(matrix[0], low) + dot(matrix[1], high))
        grad[c] = total
        rounded = total.astype(jnp.bfloat16)
        for b in range(blocks):
            lanes = slice(b * ROWB, (b + 1) * ROWB)
            for part in range(XSPLIT):
                rows = slice(part * run, (part + 1) * run)
                place = slice(part * ROWB, (part + 1) * ROWB)
                carried[b, c * run : (c + 1) * run, place] = high[rows, lanes]
                if 0 < part < XSPLIT - 1:
                    slopes[b, c * run : (c + 1) * run, place] = rounded[rows, lanes]

    for entry in shared:
        for k in near_first:
            share_line(entry, k).wait_recv()

    owner_of = [owners[0, row * blocks + b] for b in range(blocks)]
    depth = 2 * ROWB
    place_id = lax.broadcasted_iota(jnp.int32, (depth, particles), 0).astype(jnp.bfloat16)
    run_id = lax.broadcasted_iota(jnp.int32, (run, particles), 0)
    one, zero = jnp.ones((), jnp.bfloat16), jnp.zeros((), jnp.bfloat16)

    def steps_from(owner):
        slot_y = lax.rem(row_y - lax.div(owner, side) + side, side)
        slot_x = lax.rem(row_x - lax.rem(owner, side) + side, side)
        return slot_y, slot_x

    def chosen(values, within):
        here = run_id == within
        parts = []
        for f in range(components):
            kept = jnp.where(here, values[f * run : (f + 1) * run], 0.0)
            parts.append(jnp.sum(kept.reshape(run // 8, 8, particles), 0))
        return parts

    def decode(cell):
        line = third(lax.shift_right_logical(cell, 6))
        x = cell - line * x_cells
        source = lax.shift_right_logical(line, 7)
        line = line & (ROWB - 1)
        part = third(lax.shift_right_logical(x, (run // 3).bit_length() - 1))
        within = x - part * run
        return source, part * ROWB + line, within

    @pl.loop(0, blocks)
    def _(b):
        slot_y, slot_x = steps_from(owners[0, row * blocks + b])
        source, place, within = decode(cells[slot_y, slot_x])
        weight = weights[slot_x, slot_y]
        sums = [jnp.zeros((8, particles), jnp.float32) for _ in range(components)]
        for s in range(STEN):
            ones = []
            for start in range(0, XSPLIT * ROWB, depth):
                key = (place[s : s + 1] - start).astype(jnp.bfloat16)
                ones.append(jnp.where(place_id == key, one, zero))
            ones = jnp.concatenate(ones, 0)
            hot[b * STEN + s] = ones
            values = jnp.dot(carried[b], ones, preferred_element_type=jnp.float32)
            value = chosen(values, within[s : s + 1])
            for c in range(components):
                sums[c] += weight[s : s + 1] * value[c]
        for c in range(components):
            picked[b, c] = sums[c]

    for way in range(2):
        halo_copy(way).wait_recv()
    for c in range(components):
        for way, end, sign in ((0, 0, 1.0), (1, x_cells - 1, -1.0)):
            grad[c, end : end + 1, :] += (sign * NEAR) * halo_in[way, 4 + c : 5 + c, :]
            for b in range(blocks):
                lanes = slice(b * ROWB, (b + 1) * ROWB)
                far = (sign * TAIL * RATIO) * halo_in[way, c : c + 1, lanes]
                total = grad[c, edge[way], lanes] + decay[edge[way], :] * far
                grad[c, edge[way], lanes] = total
                part = way * (XSPLIT - 1)
                slopes[b, c * run : (c + 1) * run, part * ROWB : (part + 1) * ROWB] = total.astype(
                    jnp.bfloat16
                )

    @pl.loop(0, blocks)
    def _(b):
        owner = owners[0, row * blocks + b]
        rank = jnp.int32(0)
        for other in range(blocks):
            same = jnp.where(owner_of[other] == owner, 1, 0)
            rank += same * jnp.where(other < b, 1, 0)
        slot_y, slot_x = steps_from(owner)
        source, _, within = decode(cells[slot_y, slot_x])
        weight = weights[slot_x, slot_y] * offsets[slot_x, slot_y]
        sums = [picked[b, c] for c in range(components)]
        for s in range(STEN):
            values = jnp.dot(
                slopes[b], hot[b * STEN + s], preferred_element_type=jnp.float32
            )
            slope = chosen(values, within[s : s + 1])
            for c in range(components):
                sums[c] += weight[s : s + 1] * slope[c]
        mine = source[0:1] == row * CAP + rank
        for c in range(components):
            total = jnp.sum(sums[c], 0, keepdims=True)
            result[b, c : c + 1, :] = jnp.where(mine, total, 0.0)

    for step in [*farthest_first, 0]:
        to = peer(step)
        total = jnp.zeros(result.shape[1:], jnp.float32)
        for b in range(blocks):
            total += result[b] * jnp.where(owner_of[b] == to, 1.0, 0.0)
        back_out[step] = total
    for step in farthest_first:
        give_back(step).start()

    @pl.loop(1, peers)
    def _(step):
        give_back(step).wait()

    total = back_out[0]
    for step in range(1, peers):
        total += back_in[step]
    lane = lax.broadcasted_iota(jnp.int32, (1, PSIZE), 1)
    alive = jnp.concatenate(
        [jnp.where(lane < live[0, k], 1, 0) for k in range(particles // PSIZE)], 1
    )
    old = particle[...]
    total = jnp.where(alive == 1, total, 0.0)
    fluid[...] = total
    updated[...] = jnp.where(alive == 1, old + relax[...] * (total - old), old)
    for way in range(2):
        halo_copy(way).wait_send()
    for entry in shared:
        for k in near_first:
            share(entry, k).wait_send()
            share_line(entry, k).wait_send()


def put_out(grad, fluid, updated, grad_out, fluid_out, updated_out, sems):
    copies = [pltpu.make_async_copy(grad.at[c], grad_out.at[c], sems.at[c]) for c in range(3)]
    copies.append(pltpu.make_async_copy(fluid, fluid_out, sems.at[3]))
    copies.append(pltpu.make_async_copy(updated, updated_out, sems.at[4]))
    for copy in copies:
        copy.start()
    for copy in copies:
        copy.wait()


def per_device(
    ring,
    side,
    velocity,
    row_owner,
    cell_list,
    weights,
    offsets,
    relax_rate,
    particle_velocity,
    live_counts,
):
    components, x_cells, lines = velocity.shape
    blocks = lines // ROWB
    particles = weights.shape[1]
    peers = side * side
    run = x_cells // XSPLIT
    far = pl.BlockSpec(memory_space=pltpu.HBM)
    near = pl.BlockSpec(memory_space=pltpu.VMEM)
    dma = pltpu.SemaphoreType.DMA
    results = pl.pallas_call(
        functools.partial(kernel, ring, side),
        out_shape=(
            jax.ShapeDtypeStruct(velocity.shape, jnp.float32),
            jax.ShapeDtypeStruct((components, particles), jnp.float32),
            jax.ShapeDtypeStruct((components, particles), jnp.float32),
        ),
        in_specs=[far] * 10,
        out_specs=(near, near, near),
        scratch_shapes=[
            pltpu.SMEM(row_owner.shape, jnp.int32),
            pltpu.VMEM(velocity.shape, jnp.float32),
            pltpu.VMEM((2, x_cells, x_cells), jnp.bfloat16),
            pltpu.VMEM((x_cells, ROWB), jnp.float32),
            pltpu.VMEM((blocks, components * run, XSPLIT * ROWB), jnp.bfloat16),
            pltpu.VMEM((blocks, components * run, XSPLIT * ROWB), jnp.bfloat16),
            pltpu.VMEM((blocks * STEN, XSPLIT * ROWB, particles), jnp.bfloat16),
            pltpu.VMEM((2, 8, lines), jnp.float32),
            pltpu.VMEM((2, 8, lines), jnp.float32),
            pltpu.VMEM((side, side, STEN, particles), jnp.int32),
            pltpu.VMEM((side, side, STEN, particles), jnp.float32),
            pltpu.VMEM((side, side, 1, particles), jnp.float32),
            pltpu.VMEM((1, particles), jnp.float32),
            pltpu.VMEM((components, particles), jnp.float32),
            pltpu.SMEM((1, particles // PSIZE), jnp.int32),
            pltpu.VMEM((blocks, components, 8, particles), jnp.float32),
            pltpu.VMEM((blocks, components, particles), jnp.float32),
            pltpu.VMEM((peers, components, particles), jnp.float32),
            pltpu.VMEM((peers, components, particles), jnp.float32),
            pltpu.SemaphoreType.REGULAR((2,)),
            dma((12,)),
            dma((2,)),
            dma((2,)),
        ]
        + [dma((2, side))] * 6
        + [dma((peers,))] * 2,
        compiler_params=pltpu.CompilerParams(
            collective_id=0, has_side_effects=True, vmem_limit_bytes=48 * 1024 * 1024
        ),
    )(
        *(
            pltpu.with_memory_space_constraint(array, pltpu.HBM)
            for array in (
                row_owner,
                velocity,
                cell_list,
                weights,
                offsets[None],
                relax_rate[None],
                particle_velocity,
                live_counts[None],
                jnp.asarray(response_matrix(x_cells)),
                jnp.asarray(decay_table(x_cells)),
            )
        ),
    )
    return pl.pallas_call(
        put_out,
        out_shape=tuple(jax.ShapeDtypeStruct(r.shape, r.dtype) for r in results),
        in_specs=[pl.BlockSpec(memory_space=pl.ANY)] * 3,
        out_specs=(far,) * 3,
        scratch_shapes=[dma((5,))],
        compiler_params=pltpu.CompilerParams(vmem_limit_bytes=4 * 1024 * 1024),
    )(*results)


def solution(mesh):
    side = math.isqrt(mesh.shape["gy"])
    return jax.shard_map(
        functools.partial(per_device, mesh.shape["gx"], side),
        mesh=mesh,
        in_specs=(
            P(None, "gx", "gy"),
            P("gx", None),
            P(None, ("gx", "gy")),
            P(None, ("gx", "gy")),
            P(("gx", "gy")),
            P(("gx", "gy")),
            P(None, ("gx", "gy")),
            P(("gx", "gy")),
        ),
        out_specs=(P(None, "gx", "gy"), P(None, ("gx", "gy")), P(None, ("gx", "gy"))),
        check_vma=False,
    )
```

time: 29.3 us -> 26.3 us (0.90)
  the two profiles are of different devices: /device:TPU:4 before, /device:TPU:2 now
where the time goes in v2:
time: 26.3 us; the launch traced here: 26.2 us
  Pallas kernels  25.6 us (97%)
  between operations  0.64 us (2%)
    pallas_call x1, Pallas kernels, per_device(): pl.pallas_call(functools.partial(kernel, ring, side), out_shape=(jax.Shap...  24.5 us
    pallas_call x1, Pallas kernels, per_device(): pl.pallas_call(put_out, out_shape=tuple((jax.ShapeDtypeStruct(r.shape, r....  1.06 us

profile of v2, /device:TPU:2, one launch (start us, length us, event | category | flops | bytes accessed | tf_op | source)
XLA Modules:
  0.0 26.2 jit_solution(11795650603156184637)
XLA Ops:
  0.6 24.5 %shard_map.121 = (f32[3,192,512]{2,1,0:T(8,128)S(1)}, f32[3,512]{1,0:T(4,128)S(1)}, f32[3,512]{1,0:T(4,128)S(1)}) custom-call(s32[1,64]{1,0:T(1,128)} %owner_ref.1, f32[3,192,512]{2,1,0:T(8,128)} %vel_ref.1, s32[4,512]{1,0:T(4,128)} %cells_ref.1, f32[4,512]{1,0:T(4,128)} %weights_ref.1, f32[1,512]{1,0:T(1,128)} %bitcast.3, f32[1,512]{1,0:T(1,128)} %bitcast.4, ...), custom_call_target="tpu_custom_call" | custom-call | tf_op jit(solution)/shard_map/pallas_call | solution.py:439
  25.1 1.1 %shard_map.122 = (f32[3,192,512]{2,1,0:T(8,128)}, f32[3,512]{1,0:T(4,128)}, f32[3,512]{1,0:T(4,128)}) custom-call(f32[3,192,512]{2,1,0:T(8,128)S(1)} %get-tuple-element.6.grad, f32[3,512]{1,0:T(4,128)S(1)} %get-tuple-element.7.fluid, f32[3,512]{1,0:T(4,128)S(1)} %get-tuple-element.8.updated), custom_call_target="tpu_custom_call" | custom-call | tf_op jit(solution)/shard_map/pallas_call | solution.py:495

commit v3 on v2

--- a/solution.py
+++ b/solution.py
@@ -14,6 +14,7 @@
 CAP = 2
 STEN = 4
 XSPLIT = 4
+PIECES = 4
 MESH = pl.DeviceIdType.MESH
 
 DECAY = (3.0 - math.sqrt(5.0)) / 2.0
@@ -76,9 +77,7 @@
     vel,
     matrix,
     decay,
-    carried,
-    slopes,
-    hot,
+    fields,
     halo_out,
     halo_in,
     cells,
@@ -87,7 +86,6 @@
     relax,
     particle,
     live,
-    picked,
     result,
     back_out,
     back_in,
@@ -280,61 +278,10 @@
             for part in range(XSPLIT):
                 rows = slice(part * run, (part + 1) * run)
                 place = slice(part * ROWB, (part + 1) * ROWB)
-                carried[b, c * run : (c + 1) * run, place] = high[rows, lanes]
+                fields[b, c * run : (c + 1) * run, place] = high[rows, lanes]
                 if 0 < part < XSPLIT - 1:
-                    slopes[b, c * run : (c + 1) * run, place] = rounded[rows, lanes]
-
-    for entry in shared:
-        for k in near_first:
-            share_line(entry, k).wait_recv()
-
-    owner_of = [owners[0, row * blocks + b] for b in range(blocks)]
-    depth = 2 * ROWB
-    place_id = lax.broadcasted_iota(jnp.int32, (depth, particles), 0).astype(jnp.bfloat16)
-    run_id = lax.broadcasted_iota(jnp.int32, (run, particles), 0)
-    one, zero = jnp.ones((), jnp.bfloat16), jnp.zeros((), jnp.bfloat16)
-
-    def steps_from(owner):
-        slot_y = lax.rem(row_y - lax.div(owner, side) + side, side)
-        slot_x = lax.rem(row_x - lax.rem(owner, side) + side, side)
-        return slot_y, slot_x
-
-    def chosen(values, within):
-        here = run_id == within
-        parts = []
-        for f in range(components):
-            kept = jnp.where(here, values[f * run : (f + 1) * run], 0.0)
-            parts.append(jnp.sum(kept.reshape(run // 8, 8, particles), 0))
-        return parts
-
-    def decode(cell):
-        line = third(lax.shift_right_logical(cell, 6))
-        x = cell - line * x_cells
-        source = lax.shift_right_logical(line, 7)
-        line = line & (ROWB - 1)
-        part = third(lax.shift_right_logical(x, (run // 3).bit_length() - 1))
-        within = x - part * run
-        return source, part * ROWB + line, within
-
-    @pl.loop(0, blocks)
-    def _(b):
-        slot_y, slot_x = steps_from(owners[0, row * blocks + b])
-        source, place, within = decode(cells[slot_y, slot_x])
-        weight = weights[slot_x, slot_y]
-        sums = [jnp.zeros((8, particles), jnp.float32) for _ in range(components)]
-        for s in range(STEN):
-            ones = []
-            for start in range(0, XSPLIT * ROWB, depth):
-                key = (place[s : s + 1] - start).astype(jnp.bfloat16)
-                ones.append(jnp.where(place_id == key, one, zero))
-            ones = jnp.concatenate(ones, 0)
-            hot[b * STEN + s] = ones
-            values = jnp.dot(carried[b], ones, preferred_element_type=jnp.float32)
-            value = chosen(values, within[s : s + 1])
-            for c in range(components):
-                sums[c] += weight[s : s + 1] * value[c]
-        for c in range(components):
-            picked[b, c] = sums[c]
+                    d = components + c
+                    fields[b, d * run : (d + 1) * run, place] = rounded[rows, lanes]
 
     for way in range(2):
         halo_copy(way).wait_recv()
@@ -347,9 +294,42 @@
                 total = grad[c, edge[way], lanes] + decay[edge[way], :] * far
                 grad[c, edge[way], lanes] = total
                 part = way * (XSPLIT - 1)
-                slopes[b, c * run : (c + 1) * run, part * ROWB : (part + 1) * ROWB] = total.astype(
+                d = components + c
+                fields[b, d * run : (d + 1) * run, part * ROWB : (part + 1) * ROWB] = total.astype(
                     jnp.bfloat16
                 )
+
+    for entry in shared:
+        for k in near_first:
+            share_line(entry, k).wait_recv()
+
+    owner_of = [owners[0, row * blocks + b] for b in range(blocks)]
+    depth = 2 * ROWB
+    place_id = lax.broadcasted_iota(jnp.int32, (depth, particles), 0).astype(jnp.bfloat16)
+    run_id = lax.broadcasted_iota(jnp.int32, (run, particles), 0)
+    one, zero = jnp.ones((), jnp.bfloat16), jnp.zeros((), jnp.bfloat16)
+
+    def steps_from(owner):
+        slot_y = lax.rem(row_y - lax.div(owner, side) + side, side)
+        slot_x = lax.rem(row_x - lax.rem(owner, side) + side, side)
+        return slot_y, slot_x
+
+    def chosen(values, within):
+        here = run_id == within
+        parts = []
+        for f in range(2 * components):
+            kept = jnp.where(here, values[f * run : (f + 1) * run], 0.0)
+            parts.append(jnp.sum(kept.reshape(run // 8, 8, particles), 0))
+        return parts
+
+    def decode(cell):
+        line = third(lax.shift_right_logical(cell, 6))
+        x = cell - line * x_cells
+        source = lax.shift_right_logical(line, 7)
+        line = line & (ROWB - 1)
+        part = third(lax.shift_right_logical(x, (run // 3).bit_length() - 1))
+        within = x - part * run
+        return source, part * ROWB + line, within
 
     @pl.loop(0, blocks)
     def _(b):
@@ -359,16 +339,21 @@
             same = jnp.where(owner_of[other] == owner, 1, 0)
             rank += same * jnp.where(other < b, 1, 0)
         slot_y, slot_x = steps_from(owner)
-        source, _, within = decode(cells[slot_y, slot_x])
-        weight = weights[slot_x, slot_y] * offsets[slot_x, slot_y]
-        sums = [picked[b, c] for c in range(components)]
+        source, place, within = decode(cells[slot_y, slot_x])
+        weight = weights[slot_x, slot_y]
+        offset = offsets[slot_x, slot_y]
+        sums = [jnp.zeros((8, particles), jnp.float32) for _ in range(components)]
         for s in range(STEN):
+            ones = []
+            for start in range(0, XSPLIT * ROWB, depth):
+                key = (place[s : s + 1] - start).astype(jnp.bfloat16)
+                ones.append(jnp.where(place_id == key, one, zero))
             values = jnp.dot(
-                slopes[b], hot[b * STEN + s], preferred_element_type=jnp.float32
+                fields[b], jnp.concatenate(ones, 0), preferred_element_type=jnp.float32
             )
-            slope = chosen(values, within[s : s + 1])
+            parts = chosen(values, within[s : s + 1])
             for c in range(components):
-                sums[c] += weight[s : s + 1] * slope[c]
+                sums[c] += weight[s : s + 1] * (parts[c] + offset * parts[components + c])
         mine = source[0:1] == row * CAP + rank
         for c in range(components):
             total = jnp.sum(sums[c], 0, keepdims=True)
@@ -407,9 +392,13 @@
 
 
 def put_out(grad, fluid, updated, grad_out, fluid_out, updated_out, sems):
-    copies = [pltpu.make_async_copy(grad.at[c], grad_out.at[c], sems.at[c]) for c in range(3)]
-    copies.append(pltpu.make_async_copy(fluid, fluid_out, sems.at[3]))
-    copies.append(pltpu.make_async_copy(updated, updated_out, sems.at[4]))
+    pairs = [(fluid, fluid_out), (updated, updated_out)]
+    rows = grad.shape[1] // PIECES
+    for c in range(grad.shape[0]):
+        for k in range(PIECES):
+            piece = (c, pl.ds(k * rows, rows))
+            pairs.append((grad.at[piece], grad_out.at[piece]))
+    copies = [pltpu.make_async_copy(*pair, sems.at[i]) for i, pair in enumerate(pairs)]
     for copy in copies:
         copy.start()
     for copy in copies:
@@ -450,9 +439,7 @@
             pltpu.VMEM(velocity.shape, jnp.float32),
             pltpu.VMEM((2, x_cells, x_cells), jnp.bfloat16),
             pltpu.VMEM((x_cells, ROWB), jnp.float32),
-            pltpu.VMEM((blocks, components * run, XSPLIT * ROWB), jnp.bfloat16),
-            pltpu.VMEM((blocks, components * run, XSPLIT * ROWB), jnp.bfloat16),
-            pltpu.VMEM((blocks * STEN, XSPLIT * ROWB, particles), jnp.bfloat16),
+            pltpu.VMEM((blocks, 2 * components * run, XSPLIT * ROWB), jnp.bfloat16),
             pltpu.VMEM((2, 8, lines), jnp.float32),
             pltpu.VMEM((2, 8, lines), jnp.float32),
             pltpu.VMEM((side, side, STEN, particles), jnp.int32),
@@ -461,7 +448,6 @@
             pltpu.VMEM((1, particles), jnp.float32),
             pltpu.VMEM((components, particles), jnp.float32),
             pltpu.SMEM((1, particles // PSIZE), jnp.int32),
-            pltpu.VMEM((blocks, components, 8, particles), jnp.float32),
             pltpu.VMEM((blocks, components, particles), jnp.float32),
             pltpu.VMEM((peers, components, particles), jnp.float32),
             pltpu.VMEM((peers, components, particles), jnp.float32),
@@ -497,7 +483,7 @@
         out_shape=tuple(jax.ShapeDtypeStruct(r.shape, r.dtype) for r in results),
         in_specs=[pl.BlockSpec(memory_space=pl.ANY)] * 3,
         out_specs=(far,) * 3,
-        scratch_shapes=[dma((5,))],
+        scratch_shapes=[dma((2 + components * PIECES,))],
         compiler_params=pltpu.CompilerParams(vmem_limit_bytes=4 * 1024 * 1024),
     )(*results)
 

time: 26.3 us -> 25.5 us (0.970)
  Pallas kernels: 25.6 us -> 24.7 us
    pallas_call x1, Pallas kernels: 24.5 us -> 23.6 us  [per_device(): pl.pallas_call(functools.partial(kernel, ring, side), out_shape=(jax.Shap...]
where the time goes in v3:
time: 25.5 us; the launch traced here: 25.3 us
  Pallas kernels  24.7 us (97%)
  between operations  0.64 us (3%)
    pallas_call x1, Pallas kernels, per_device(): pl.pallas_call(functools.partial(kernel, ring, side), out_shape=(jax.Shap...  23.6 us
    pallas_call x1, Pallas kernels, per_device(): pl.pallas_call(put_out, out_shape=tuple((jax.ShapeDtypeStruct(r.shape, r....  1.13 us

profile of v3, /device:TPU:2, one launch (start us, length us, event | category | flops | bytes accessed | tf_op | source)
XLA Modules:
  0.0 25.3 jit_solution(14846279877741577204)
XLA Ops:
  0.6 23.6 %shard_map.121 = (f32[3,192,512]{2,1,0:T(8,128)S(1)}, f32[3,512]{1,0:T(4,128)S(1)}, f32[3,512]{1,0:T(4,128)S(1)}) custom-call(s32[1,64]{1,0:T(1,128)} %owner_ref.1, f32[3,192,512]{2,1,0:T(8,128)} %vel_ref.1, s32[4,512]{1,0:T(4,128)} %cells_ref.1, f32[4,512]{1,0:T(4,128)} %weights_ref.1, f32[1,512]{1,0:T(1,128)} %bitcast.3, f32[1,512]{1,0:T(1,128)} %bitcast.4, ...), custom_call_target="tpu_custom_call" | custom-call | tf_op jit(solution)/shard_map/pallas_call | solution.py:428
  24.2 1.1 %shard_map.122 = (f32[3,192,512]{2,1,0:T(8,128)}, f32[3,512]{1,0:T(4,128)}, f32[3,512]{1,0:T(4,128)}) custom-call(f32[3,192,512]{2,1,0:T(8,128)S(1)} %get-tuple-element.6.grad, f32[3,512]{1,0:T(4,128)S(1)} %get-tuple-element.7.fluid, f32[3,512]{1,0:T(4,128)S(1)} %get-tuple-element.8.updated), custom_call_target="tpu_custom_call" | custom-call | tf_op jit(solution)/shard_map/pallas_call | solution.py:481

commit v4 on v3

--- a/solution.py
+++ b/solution.py
@@ -14,7 +14,7 @@
 CAP = 2
 STEN = 4
 XSPLIT = 4
-PIECES = 4
+PIECES = 1
 MESH = pl.DeviceIdType.MESH
 
 DECAY = (3.0 - math.sqrt(5.0)) / 2.0
@@ -256,13 +256,6 @@
         for k in near_first:
             share_line(entry, k).start()
 
-    for way in range(2):
-
-        @pl.when(leads[way] == 1)
-        def _(way=way):
-            pl.semaphore_wait(ready.at[way], 1)
-            halo_copy(way).start()
-
     for load in loads[6:]:
         load.wait()
     for c in range(components):
@@ -282,6 +275,13 @@
                 if 0 < part < XSPLIT - 1:
                     d = components + c
                     fields[b, d * run : (d + 1) * run, place] = rounded[rows, lanes]
+
+    for way in range(2):
+
+        @pl.when(leads[way] == 1)
+        def _(way=way):
+            pl.semaphore_wait(ready.at[way], 1)
+            halo_copy(way).start()
 
     for way in range(2):
         halo_copy(way).wait_recv()
@@ -368,27 +368,27 @@
     for step in farthest_first:
         give_back(step).start()
 
-    @pl.loop(1, peers)
-    def _(step):
-        give_back(step).wait()
-
-    total = back_out[0]
-    for step in range(1, peers):
-        total += back_in[step]
-    lane = lax.broadcasted_iota(jnp.int32, (1, PSIZE), 1)
-    alive = jnp.concatenate(
-        [jnp.where(lane < live[0, k], 1, 0) for k in range(particles // PSIZE)], 1
-    )
-    old = particle[...]
-    total = jnp.where(alive == 1, total, 0.0)
-    fluid[...] = total
-    updated[...] = jnp.where(alive == 1, old + relax[...] * (total - old), old)
     for way in range(2):
         halo_copy(way).wait_send()
     for entry in shared:
         for k in near_first:
             share(entry, k).wait_send()
             share_line(entry, k).wait_send()
+    lane = lax.broadcasted_iota(jnp.int32, (1, PSIZE), 1)
+    alive = jnp.concatenate(
+        [jnp.where(lane < live[0, k], 1, 0) for k in range(particles // PSIZE)], 1
+    )
+    old = particle[...]
+    rate = relax[...]
+    total = back_out[0]
+    for step in reversed(farthest_first):
+        give_back(step).wait_send()
+    for step in reversed(farthest_first):
+        give_back(step).wait_recv()
+        total += back_in[step]
+    total = jnp.where(alive == 1, total, 0.0)
+    fluid[...] = total
+    updated[...] = jnp.where(alive == 1, old + rate * (total - old), old)
 
 
 def put_out(grad, fluid, updated, grad_out, fluid_out, updated_out, sems):

time: 25.5 us -> 25.3 us (level)
  no operation moved by 1% of the time
where the time goes in v4:
time: 25.3 us; the launch traced here: 25.2 us
  Pallas kernels  24.6 us (97%)
  between operations  0.64 us (3%)
    pallas_call x1, Pallas kernels, per_device(): pl.pallas_call(functools.partial(kernel, ring, side), out_shape=(jax.Shap...  23.5 us
    pallas_call x1, Pallas kernels, per_device(): pl.pallas_call(put_out, out_shape=tuple((jax.ShapeDtypeStruct(r.shape, r....  1.06 us

profile of v4, /device:TPU:2, one launch (start us, length us, event | category | flops | bytes accessed | tf_op | source)
XLA Modules:
  0.0 25.2 jit_solution(13892962045151787593)
XLA Ops:
  0.6 23.5 %shard_map.121 = (f32[3,192,512]{2,1,0:T(8,128)S(1)}, f32[3,512]{1,0:T(4,128)S(1)}, f32[3,512]{1,0:T(4,128)S(1)}) custom-call(s32[1,64]{1,0:T(1,128)} %owner_ref.1, f32[3,192,512]{2,1,0:T(8,128)} %vel_ref.1, s32[4,512]{1,0:T(4,128)} %cells_ref.1, f32[4,512]{1,0:T(4,128)} %weights_ref.1, f32[1,512]{1,0:T(1,128)} %bitcast.3, f32[1,512]{1,0:T(1,128)} %bitcast.4, ...), custom_call_target="tpu_custom_call" | custom-call | tf_op jit(solution)/shard_map/pallas_call | solution.py:428
  24.1 1.1 %shard_map.122 = (f32[3,192,512]{2,1,0:T(8,128)}, f32[3,512]{1,0:T(4,128)}, f32[3,512]{1,0:T(4,128)}) custom-call(f32[3,192,512]{2,1,0:T(8,128)S(1)} %get-tuple-element.6.grad, f32[3,512]{1,0:T(4,128)S(1)} %get-tuple-element.7.fluid, f32[3,512]{1,0:T(4,128)S(1)} %get-tuple-element.8.updated), custom_call_target="tpu_custom_call" | custom-call | tf_op jit(solution)/shard_map/pallas_call | solution.py:481

commit v5 on v4

--- a/solution.py
+++ b/solution.py
@@ -359,13 +359,16 @@
             total = jnp.sum(sums[c], 0, keepdims=True)
             result[b, c : c + 1, :] = jnp.where(mine, total, 0.0)
 
-    for step in [*farthest_first, 0]:
+    lag = 6
+    for i, step in enumerate([*farthest_first, 0]):
         to = peer(step)
         total = jnp.zeros(result.shape[1:], jnp.float32)
         for b in range(blocks):
             total += result[b] * jnp.where(owner_of[b] == to, 1.0, 0.0)
         back_out[step] = total
-    for step in farthest_first:
+        if i >= lag:
+            give_back(farthest_first[i - lag]).start()
+    for step in farthest_first[max(peers - lag, 0) :]:
         give_back(step).start()
 
     for way in range(2):

time: 25.3 us -> 25.3 us (level)
  no operation moved by 1% of the time
where the time goes in v5:
time: 25.3 us; the launch traced here: 25.2 us
  Pallas kernels  24.5 us (97%)
  between operations  0.64 us (3%)
    pallas_call x1, Pallas kernels, per_device(): pl.pallas_call(functools.partial(kernel, ring, side), out_shape=(jax.Shap...  23.5 us
    pallas_call x1, Pallas kernels, per_device(): pl.pallas_call(put_out, out_shape=tuple((jax.ShapeDtypeStruct(r.shape, r....  1.06 us

profile of v5, /device:TPU:2, one launch (start us, length us, event | category | flops | bytes accessed | tf_op | source)
XLA Modules:
  0.0 25.2 jit_solution(9991463302333922206)
XLA Ops:
  0.6 23.5 %shard_map.121 = (f32[3,192,512]{2,1,0:T(8,128)S(1)}, f32[3,512]{1,0:T(4,128)S(1)}, f32[3,512]{1,0:T(4,128)S(1)}) custom-call(s32[1,64]{1,0:T(1,128)} %owner_ref.1, f32[3,192,512]{2,1,0:T(8,128)} %vel_ref.1, s32[4,512]{1,0:T(4,128)} %cells_ref.1, f32[4,512]{1,0:T(4,128)} %weights_ref.1, f32[1,512]{1,0:T(1,128)} %bitcast.3, f32[1,512]{1,0:T(1,128)} %bitcast.4, ...), custom_call_target="tpu_custom_call" | custom-call | tf_op jit(solution)/shard_map/pallas_call | solution.py:431
  24.1 1.1 %shard_map.122 = (f32[3,192,512]{2,1,0:T(8,128)}, f32[3,512]{1,0:T(4,128)}, f32[3,512]{1,0:T(4,128)}) custom-call(f32[3,192,512]{2,1,0:T(8,128)S(1)} %get-tuple-element.6.grad, f32[3,512]{1,0:T(4,128)S(1)} %get-tuple-element.7.fluid, f32[3,512]{1,0:T(4,128)S(1)} %get-tuple-element.8.updated), custom_call_target="tpu_custom_call" | custom-call | tf_op jit(solution)/shard_map/pallas_call | solution.py:484
